TPU v7x, 512 devices: a whole 4x4x16 slice. The times are simulated.
512 devices in a mesh: dp: 4 (over x), fsdp: 4 (over y_hi, core), tensor: 32 (over z, y_lo).
Axes of the slice: x: 4, y: 4 (y_hi: 2, y_lo: 2; y = y_hi * 2 + y_lo), z: 16, core: 2. Of those that a mesh axis runs over, the one named last changes fastest.
Arguments:
- activations: bfloat16 [4096, 4096], P(('dp', 'tensor'), 'fsdp'), may hold values from -6 to 6
- cotangent: bfloat16 [4096, 16384], P('dp', 'tensor'), may hold values from -6 to 6
- weight: bfloat16 [4096, 16384], P('fsdp', 'tensor'), may hold values from -0.046875 to 0.046875
- residual: bfloat16 [4, 4096, 16384], P('dp', 'fsdp', 'tensor'), may hold values from -6 to 6
- step_size: float32 [1], replicated, may hold values from 0.02 to 0.06
- kept_blocks: int32 [4, 4, 32, 8], P('dp', 'fsdp', 'tensor'), may hold values from 0 to 31, as said below
Outputs:
- input_grad: bfloat16 [4096, 4096], P(('dp', 'tensor'), 'fsdp')
- residual_out: bfloat16 [4, 4096, 16384], P('dp', 'fsdp', 'tensor')
- owned: float32 [4, 4, 32, 8, 128, 128], P('dp', 'fsdp', 'tensor')
Inputs may be any that keep to these rules, and one draw needn't show every extreme that they name: The 8 entries of kept_blocks[a, f, t, :] are different block numbers.
All inputs are finite; a program needn't handle non-finite values.
Results may differ from a plain program's by a relative error of at most 0.0029.
Values may be sent and summed in bfloat16 or wider, within the bound.
A program may use at most 64 MiB of HBM per device.

v0:
```python
import jax
import jax.numpy as jnp
from jax import lax
from jax.sharding import Mesh
from jax.sharding import PartitionSpec as P

BLK = 128
TENSOR = ("tensor_0", "tensor_1")
DP_TENSOR = ("dp", "tensor_0", "tensor_1")


def whole_of(x, axes, dim):
    for axis in reversed(axes):
        x = lax.all_gather(x, axis, axis=dim, tiled=True)
    return x


def own_rows(total, axes):
    for axis in axes:
        total = lax.psum_scatter(total, axis, scatter_dimension=0, tiled=True)
    return total


def body(activations, cotangent, weight, residual, step_size, kept_blocks):
    width_rows = weight.shape[0]
    width_cols = weight.shape[1]
    row_block_count = width_rows // BLK
    col_blocks = width_cols // BLK
    count = row_block_count * col_blocks
    groups = lax.axis_size("dp")
    matching = cotangent
    gradient = lax.dot_general(
        whole_of(activations, TENSOR, 0),
        matching,
        (((0,), (0,)), ((), ())),
        preferred_element_type=jnp.float32,
    )
    matching = cotangent
    summed = own_rows(
        lax.dot_general(
            matching, weight, (((1,), (1,)), ((), ())), preferred_element_type=jnp.float32
        ),
        TENSOR,
    )
    input_grad = summed.astype(jnp.bfloat16)
    accumulated = residual[0].astype(jnp.float32) + step_size[0] * gradient
    rounded = accumulated.astype(jnp.bfloat16)
    choices_here = kept_blocks.reshape(-1)
    keep_count = choices_here.shape[0]
    block_numbers = jnp.arange(count, dtype=jnp.int32)
    chosen = jnp.any(block_numbers[:, None] == choices_here[None, :], axis=1).reshape(
        row_block_count, 1, col_blocks, 1
    )
    zero = jnp.zeros((), jnp.bfloat16)
    shaped = rounded.reshape(row_block_count, BLK, col_blocks, BLK)
    residual_out = jnp.where(chosen, zero, shaped).reshape(1, width_rows, width_cols)

    def take_block(number):
        return lax.dynamic_slice(
            rounded, (number // col_blocks * BLK, number % col_blocks * BLK), (BLK, BLK)
        )

    blocks = jax.vmap(take_block)(choices_here).reshape(keep_count, BLK * BLK)
    owners = choices_here % groups
    places = choices_here // groups
    owned_count = count // groups
    position = jnp.arange(keep_count, dtype=jnp.int32)
    earlier = (owners[:, None] == owners[None, :]) & (position[None, :] < position[:, None])
    slot_index = jnp.sum(earlier.astype(jnp.int32), axis=1)
    target_row = owners * keep_count + slot_index
    all_rows = jnp.arange(groups * keep_count, dtype=jnp.int32)
    placing = all_rows[:, None] == target_row[None, :]
    outgoing = jnp.dot(
        placing.astype(jnp.bfloat16), blocks, preferred_element_type=jnp.float32
    ).astype(jnp.bfloat16)
    outgoing = outgoing.reshape(groups, keep_count, BLK * BLK)
    labels = jnp.sum(placing.astype(jnp.int32) * (places + 1)[None, :], axis=1) - 1
    labels = labels.reshape(groups, keep_count)
    arrived, arrived_labels = (
        lax.all_to_all(outgoing, "dp", split_axis=0, concat_axis=0, tiled=True),
        lax.all_to_all(labels, "dp", split_axis=0, concat_axis=0, tiled=True),
    )
    arrived = arrived.reshape(groups * keep_count, BLK * BLK)
    owned_numbers = jnp.arange(owned_count, dtype=jnp.int32)
    matching = owned_numbers[:, None] == arrived_labels.reshape(-1)[None, :]
    owned = jnp.dot(matching.astype(jnp.bfloat16), arrived, preferred_element_type=jnp.float32)
    owned = owned.reshape(1, 1, 1, owned_count, BLK, BLK)
    return (input_grad, residual_out, owned)


def solution(mesh):
    split = Mesh(
        mesh.devices.reshape(mesh.shape["dp"], mesh.shape["fsdp"], 16, 2),
        ("dp", "fsdp", "tensor_0", "tensor_1"),
    )
    return jax.shard_map(
        body,
        mesh=split,
        in_specs=(
            P(DP_TENSOR, "fsdp"),
            P("dp", TENSOR),
            P("fsdp", TENSOR),
            P("dp", "fsdp", TENSOR),
            P(),
            P("dp", "fsdp", TENSOR, None),
        ),
        out_specs=(
            P(DP_TENSOR, "fsdp"),
            P("dp", "fsdp", TENSOR),
            P("dp", "fsdp", TENSOR, None, None, None),
        ),
        check_vma=False,
    )
```

profile of v0, /device:TPU:1, one launch (start us, length us, event | category | flops | bytes accessed | tf_op | source)
XLA Modules:
  0.0 202.1 jit_solution(10703023676564604675)
XLA Ops:
  7.2 6.3 %all_gather.6 = bf16[64,1024]{1,0:T(8,128)(2,1)} all-gather(bf16[32,1024]{1,0:T(8,128)(2,1)} %param.6), channel_id=1, replica_groups=mesh['dp'=4,'fsdp'=4,'tensor_0'=16,'tensor_1'=2] {'tensor_1'}, dimensions={0}, use_global_device_ids=true | all-gather | bytes 196608 | tf_op jit(solution)/shard_map/all_gather | solution.py:14
  13.6 4.4 %fusion.16 = f32[1024,1024]{1,0:T(8,128)} fusion(bf16[1024,512]{1,0:T(8,128)(2,1)S(1)} %copy-done, bf16[1024,512]{1,0:T(8,128)(2,1)} %param.8), kind=kOutput, calls=%fused_computation.43 | convolution fusion | flops 1073741824 | bytes 6291456 | tf_op jit(solution)/shard_map/dot_general | solution.py:40
  18.1 0.6 copy-done.2
  18.7 0.2 convert_reduce_fusion
  18.9 0.1 select_reduce_fusion
  19.0 0.7 sub.16
  19.7 4.0 %all-to-all-start = ((s32[4,1,8]{2,1,0:T(1,128)}), s32[4,1,8]{2,1,0:T(1,128)S(1)}, u32[]{:S(2)}, u32[]{:S(2)}) async-start(s32[4,1,8]{2,1,0:T(1,128)} %bitcast.4), calls=%async_computation.2 | async-start | bytes 4096 | tf_op jit(solution)/shard_map/all_to_all | solution.py:81
  24.4 57.8 %all-gather.2.cloned.1.call-done = bf16[1024,1024]{1,0:T(8,128)(2,1)} async-done(((bf16[64,1024]{1,0:T(8,128)(2,1)}), bf16[1024,1024]{1,0:T(8,128)(2,1)}) %all-gather.2.cloned.1.call-update) | async-done | bytes 2097168 | tf_op jit(solution)/shard_map/all_gather | solution.py:14
  82.2 2.9 %fusion.1 = bf16[1024,512]{1,0:T(8,128)(2,1)S(1)} fusion(bf16[1024,1024]{1,0:T(8,128)(2,1)} %all-gather.2.cloned.1.call-done, bf16[1024,512]{1,0:T(8,128)(2,1)S(1)} %copy-done, bf16[1,1024,512]{2,1,0:T(8,128)(2,1)S(1)} %copy-done.1, f32[]{:T(128)} %bitcast.74), kind=kOutput, calls=%fused_computation.5 | convolution fusion | flops 1075838976 | bytes 5242884 | tf_op jit(solution)/shard_map/dot_general | solution.py:32
  85.1 15.4 %while.1 = (s32[]{:T(128)}, bf16[1024,512]{1,0:T(8,128)(2,1)S(1)}, s32[8,2]{0,1:T(2,128)S(1)}, bf16[8,128,128]{2,1,0:T(8,128)(2,1)S(1)}, s32[]{:T(128)}) while((s32[]{:T(128)}, bf16[1024,512]{1,0:T(8,128)(2,1)S(1)}, s32[8,2]{0,1:T(2,128)S(1)}, bf16[8,128,128]{2,1,0:T(8,128)(2,1)S(1)}, s32[]{:T(128)}) %tuple.29), condition=%wide.while_cond, body=%wide.while_body.sunk | while | flops 2 | bytes 65653 | solution.py:59
  85.1 0.1 constant_dynamic-slice_fusion.2
  85.2 0.5 fusion.23
  85.7 1.3 bitcast_dynamic-update-slice_fusion.2
  87.0 0.1 constant_dynamic-slice_fusion.2
  87.1 0.5 fusion.23
  87.6 1.3 bitcast_dynamic-update-slice_fusion.2
  89.0 0.1 constant_dynamic-slice_fusion.2
  89.0 0.5 fusion.23
  89.6 1.3 bitcast_dynamic-update-slice_fusion.2
  90.9 0.1 constant_dynamic-slice_fusion.2
  91.0 0.5 fusion.23
  91.5 1.3 bitcast_dynamic-update-slice_fusion.2
  92.8 0.1 constant_dynamic-slice_fusion.2
  92.9 0.5 fusion.23
  93.4 1.3 bitcast_dynamic-update-slice_fusion.2
  94.7 0.1 constant_dynamic-slice_fusion.2
  94.8 0.5 fusion.23
  95.3 1.3 bitcast_dynamic-update-slice_fusion.2
  96.7 0.1 constant_dynamic-slice_fusion.2
  96.8 0.5 fusion.23
  97.3 1.3 bitcast_dynamic-update-slice_fusion.2
  98.6 0.1 constant_dynamic-slice_fusion.2
  98.7 0.5 fusion.23
  99.2 1.3 bitcast_dynamic-update-slice_fusion.2
  100.5 1.5 fusion
  102.1 4.0 %all-to-all-start.1 = ((bf16[4,8,16384]{2,1,0:T(8,128)(2,1)}), bf16[4,8,16384]{2,1,0:T(8,128)(2,1)S(1)}, u32[]{:S(2)}, u32[]{:S(2)}) async-start(bf16[4,8,16384]{2,1,0:T(8,128)(2,1)} %fusion), calls=%async_computation.3 | async-start | bytes 2097152 | tf_op jit(solution)/shard_map/all_to_all | solution.py:80
  106.0 55.8 %reduce-scatter.3.cloned.1.call-done = f32[64,1024]{1,0:T(8,128)} async-done(((f32[1024,1024]{1,0:T(8,128)}), f32[64,1024]{1,0:T(8,128)}) %reduce-scatter.3.cloned.1.call-update) | async-done | bytes 262160 | tf_op jit(solution)/shard_map/reduce_scatter | solution.py:20
  161.9 0.1 fusion.7
  162.0 0.1 broadcast_in_dim.16
  162.0 0.5 broadcast.331
  162.6 0.7 reduce.3
  163.2 0.1 eq.87
  163.3 0.3 broadcast_in_dim.17
  163.7 1.3 fusion.2
  164.9 0.2 convolution_bitcast_fusion
  165.2 0.9 copy.17
  166.1 28.0 %reduce-scatter.5.cloned.1.call-done = f32[32,1024]{1,0:T(8,128)} async-done(((f32[64,1024]{1,0:T(8,128)}), f32[32,1024]{1,0:T(8,128)}) %reduce-scatter.5.cloned.1.call-update) | async-done | bytes 131088 | tf_op jit(solution)/shard_map/reduce_scatter | solution.py:20
  194.0 1.5 convert_element_type.21
  (19 shorter events, 0.2 us)
Async XLA Ops:
  7.2 6.5 %copy-start = (bf16[1024,512]{1,0:T(8,128)(2,1)S(1)}, bf16[1024,512]{1,0:T(8,128)(2,1)}, u32[]{:S(2)}) copy-start(bf16[1024,512]{1,0:T(8,128)(2,1)} %param.7) | copy-start | bytes 3145732
  7.2 75.0 %all-gather.2.cloned.1.call-start = ((), (), s32[]{:S(2)}) async-start(), calls=%async_computation.6 | async-start | bytes 2228224 | tf_op jit(solution)/shard_map/all_gather | solution.py:14
  13.6 148.3 %reduce-scatter.3.cloned.1.call-start = ((), (), s32[]{:S(2)}) async-start(), calls=%async_computation.4 | async-start | bytes 4456448 | tf_op jit(solution)/shard_map/reduce_scatter | solution.py:20
  18.1 0.7 copy-start.2
  18.1 64.1 %copy-start.1 = (bf16[1,1024,512]{2,1,0:T(8,128)(2,1)S(1)}, bf16[1,1024,512]{2,1,0:T(8,128)(2,1)}, u32[]{:S(2)}) copy-start(bf16[1,1024,512]{2,1,0:T(8,128)(2,1)} %param.9) | copy-start | bytes 3145732
  19.7 82.4 %all-to-all-start = ((s32[4,1,8]{2,1,0:T(1,128)}), s32[4,1,8]{2,1,0:T(1,128)S(1)}, u32[]{:S(2)}, u32[]{:S(2)}) async-start(s32[4,1,8]{2,1,0:T(1,128)} %bitcast.4), calls=%async_computation.2 | async-start | bytes 4096 | tf_op jit(solution)/shard_map/all_to_all | solution.py:81
  102.1 62.8 %all-to-all-start.1 = ((bf16[4,8,16384]{2,1,0:T(8,128)(2,1)}), bf16[4,8,16384]{2,1,0:T(8,128)(2,1)S(1)}, u32[]{:S(2)}, u32[]{:S(2)}) async-start(bf16[4,8,16384]{2,1,0:T(8,128)(2,1)} %fusion), calls=%async_computation.3 | async-start | bytes 2097152 | tf_op jit(solution)/shard_map/all_to_all | solution.py:80
  106.0 88.0 %reduce-scatter.5.cloned.1.call-start = ((), (), s32[]{:S(2)}) async-start(), calls=%async_computation.5 | async-start | bytes 393216 | tf_op jit(solution)/shard_map/reduce_scatter | solution.py:20
Sparse Core Ops, SparseCore 0:
  13.7 68.4 all-gather.1
  85.0 76.7 reduce-scatter.2
  164.6 29.3 reduce-scatter.4
where the time goes:
time: 203 us; the launch traced here: 202 us
  waiting for transfers between devices  142 us (70%)
  local copies, waits for them, and re-layouts  18.5 us (9%)
  between operations  14.5 us (7%)
  matrix products  9.1 us (4%)
  starting transfers between devices  8.06 us (4%)
  blocking collectives  6.32 us (3%)
  other arithmetic  3.86 us (2%)
    reduce_scatter x2, waiting for transfers between devices, own_rows(): total = lax.psum_scatter(total, axis, scatter_dimension=0, tiled=True)  83.8 us
    all_gather x1, waiting for transfers between devices, whole_of(): x = lax.all_gather(x, axis, axis=dim, tiled=True)  57.8 us
    gather x24, local copies, waits for them, and re-layouts  15.3 us
    all_gather x1, blocking collectives, whole_of(): x = lax.all_gather(x, axis, axis=dim, tiled=True)  6.32 us
    dot_general x1, matrix products, body(): lax.dot_general(matching, weight, (((1,), (1,)), ((), ())), preferred_ele...  4.44 us
  transfers between devices with their start and end apart: 5, of which 3 were waited for; matrix products, arithmetic and copies ran while one was open for 15% of the time, Pallas kernels for 0%

commit v1 on v0

v1 whole, which is shorter than its diff:
```python
import functools

import jax
import jax.numpy as jnp
from jax import lax
from jax.experimental import pallas as pl
from jax.experimental.pallas import tpu as pltpu
from jax.sharding import PartitionSpec as P

BLK = 128
MESH = pl.DeviceIdType.MESH
NT = (((1,), (1,)), ((), ()))
F32 = jnp.float32
BF16 = jnp.bfloat16


def kernel(
    step_ref, kept_ref, acts_ref, cot_hbm, w_hbm, res_hbm,
    ig_ref, ro_ref, ow_ref,
    full, cot, w, res, own, yout, yin, ring, sent, dpin,
    local_sem, pair_send, pair_recv, ag_send, ag_recv, ya_send, ya_recv,
    yr_send, yr_recv, rs_send, rs_recv, dp_send, dp_recv,
):
    planes = cot.shape[0]
    half = planes // 2
    rows = cot.shape[2]
    hid = cot.shape[3]
    cols = full.shape[4]
    a = lax.axis_index("dp")
    f = lax.axis_index("fsdp")
    t = lax.axis_index("tensor")
    groups = lax.axis_size("dp")
    z = t // 2
    par = t % 2

    def plane(p):
        return lax.rem(p + 2 * planes, planes)

    up = (a, f, plane(z + 1) * 2 + par)
    down = (a, f, plane(z - 1) * 2 + par)
    pair = (a, f, z * 2 + 1 - par)
    zdev = (up, down)
    sign = (1, -1)

    def dpdev(k):
        return (lax.rem(a + k, groups), f, t)

    def remote(src, dst, send, recv, dev):
        return pltpu.make_async_remote_copy(
            src_ref=src, dst_ref=dst, send_sem=send, recv_sem=recv, device_id=dev, device_id_type=MESH
        )

    loads = [
        pltpu.make_async_copy(acts_ref.at[:, pl.ds(0, cols)], full.at[0, z, par], local_sem.at[0]),
        pltpu.make_async_copy(acts_ref.at[:, pl.ds(cols, cols)], full.at[1, z, par], local_sem.at[1]),
        pltpu.make_async_copy(cot_hbm, cot, local_sem.at[2]),
        pltpu.make_async_copy(w_hbm, w, local_sem.at[3]),
        pltpu.make_async_copy(res_hbm, res, local_sem.at[4]),
    ]
    for load in loads:
        load.start()

    barrier = pltpu.get_barrier_semaphore()
    others = [up, down, pair] + [dpdev(k) for k in range(1, groups)]
    for dev in others:
        pl.semaphore_signal(barrier, inc=1, device_id=dev, device_id_type=MESH)
    pl.semaphore_wait(barrier, len(others))

    def pair_copy():
        return remote(full.at[0, z, par], full.at[0, z, par], pair_send, pair_recv, pair)

    def pair_arrival():
        return remote(full.at[0, z, 1 - par], full.at[0, z, 1 - par], pair_send, pair_recv, pair)

    def gather_copy(h, d, s):
        p = plane(z - sign[d] * s)
        if h == 0:
            ref = full.at[0, p]
        else:
            ref = full.at[1, p, par]
        return remote(ref, ref, ag_send.at[h, d, s], ag_recv.at[h, d, s], zdev[d])

    def gather_arrival(h, d, s):
        p = plane(z - sign[d] * (s + 1))
        if h == 0:
            ref = full.at[0, p]
        else:
            ref = full.at[1, p, par]
        return remote(ref, ref, ag_send.at[h, d, s], ag_recv.at[h, d, s], zdev[d])

    def across_copy(p):
        ref = full.at[1, p, par]
        return remote(ref, ref, ya_send.at[p], ya_recv.at[p], pair)

    def across_arrival(p):
        ref = full.at[1, p, 1 - par]
        return remote(ref, ref, ya_send.at[p], ya_recv.at[p], pair)

    def exchange_plane(q):
        i = (q + 1) // 2
        return plane(z + (2 * (q % 2) - 1) * (half - i))

    def exchange_copy(p):
        return remote(yout.at[p], yin.at[p], yr_send.at[p], yr_recv.at[p], pair)

    def ring_copy(d, h, k, p):
        return remote(
            own.at[p, h], ring.at[d, h, k - 1], rs_send.at[d, h, k], rs_recv.at[d, h, k - 1], zdev[d]
        )

    def ring_arrival(d, h, k, p):
        return remote(
            own.at[p, h], ring.at[d, h, k], rs_send.at[d, h, k], rs_recv.at[d, h, k], zdev[d]
        )

    def dp_copy(k, g):
        lines = pl.ds(pl.multiple_of(g * 2 * BLK, 2 * BLK), 2 * BLK)
        return remote(
            sent.at[lax.rem(a + k, groups), lines], dpin.at[k - 1, lines],
            dp_send.at[k - 1, g], dp_recv.at[k - 1, g], dpdev(k),
        )

    def hops(h, d):
        return half if h == d else half - 1

    loads[0].wait()
    loads[1].wait()
    pair_copy().start()
    gather_copy(1, 0, 0).start()
    gather_copy(1, 1, 0).start()
    across_copy(z).start()
    loads[2].wait()
    loads[3].wait()

    def partial(b, parity):
        x = cot[pl.ds(b * half, half), parity].reshape(half * rows, hid)
        return lax.dot_general(x, w[...], NT, preferred_element_type=F32).reshape(half, rows, 2 * cols)

    def theirs(b, carry):
        y = partial(b, 1 - par).astype(BF16)
        yout[pl.ds(b * half, half), 0] = y[:, :, :cols]
        yout[pl.ds(b * half, half), 1] = y[:, :, cols:]
        return carry

    def ours(b, carry):
        y = partial(b, par)
        own[pl.ds(b * half, half), 0] = y[:, :, :cols]
        own[pl.ds(b * half, half), 1] = y[:, :, cols:]
        return carry

    theirs(0, 0)
    pair_arrival().wait_recv()
    gather_copy(0, 0, 0).start()
    gather_copy(0, 1, 0).start()
    theirs(1, 0)
    for q in range(2):
        exchange_copy(exchange_plane(q)).start()
    lax.fori_loop(0, 2, ours, 0)

    def gather_step(s, carry):
        for h in (1, 0):
            for d in range(2):
                gather_arrival(h, d, s).wait_recv()
                if h == d:
                    gather_copy(h, d, s + 1).start()
                else:
                    @pl.when(s + 1 < half - 1)
                    def _():
                        gather_copy(h, d, s + 1).start()
                if h == 1:
                    across_copy(plane(z - sign[d] * (s + 1))).start()
        exchange_copy(exchange_plane(s + 2)).start()
        return carry

    lax.fori_loop(0, half - 1, gather_step, 0)
    gather_arrival(1, 1, half - 1).wait_recv()
    across_copy(plane(z + half)).start()
    gather_arrival(0, 0, half - 1).wait_recv()

    def rest(q, carry):
        exchange_copy(exchange_plane(q)).start()
        return carry

    lax.fori_loop(half + 1, planes, rest, 0)

    def exchanged(p):
        remote(yout.at[p], yin.at[p], yr_send.at[p], yr_recv.at[p], pair).wait_recv()

    far = plane(z + half)
    exchanged(far)
    for d in range(2):
        own[far, d] = own[far, d] + yin[far, d].astype(F32)
        ring_copy(d, d, half, far).start()

    def ring_step(k, first):
        for d in range(2):
            p = plane(z + sign[d] * k)
            exchanged(p)
            for h in (d, 1 - d):
                total = own[p, h] + yin[p, h].astype(F32)
                if not (first and h != d):
                    ring_arrival(d, h, k, p).wait_recv()
                    total = total + ring[d, h, k]
                own[p, h] = total
                ring_copy(d, h, k, p).start()

    step = step_ref[0]
    kept = [kept_ref[i] for i in range(kept_ref.shape[0])]

    def gradient(g):
        h = g // 2
        lanes = pl.ds(pl.multiple_of((g % 2) * 2 * BLK, 2 * BLK), 2 * BLK)
        lines = pl.ds(pl.multiple_of(g * 2 * BLK, 2 * BLK), 2 * BLK)
        x = full[h, :, :, :, lanes].reshape(planes * 2 * rows, 2 * BLK)
        y = cot[...].reshape(planes * 2 * rows, hid)
        grad = lax.dot_general(x, y, (((0,), (0,)), ((), ())), preferred_element_type=F32)
        rounded = (res[lines].astype(F32) + step * grad).astype(BF16)
        for i in range(2):
            for o in range(groups):
                number = (2 * g + i) * groups + o
                hit = kept[0] == number
                for other in kept[1:]:
                    hit = jnp.logical_or(hit, other == number)
                keep = jnp.where(hit, 1.0, 0.0)
                block = rounded[i * BLK:(i + 1) * BLK, o * BLK:(o + 1) * BLK].astype(F32)
                here = pl.ds(pl.multiple_of((2 * g + i) * BLK, BLK), BLK)
                ro_ref[here, o * BLK:(o + 1) * BLK] = (block * (1.0 - keep)).astype(BF16)
                sent[o, here] = (block * keep).astype(BF16)
        for k in range(1, groups):
            dp_copy(k, g).start()

    ring_step(half - 1, True)
    lax.fori_loop(0, planes, lambda p, c: (across_arrival(p).wait_recv(), c)[1], 0)
    loads[4].wait()

    def both(s, carry):
        ring_step(half - 1 - s, False)

        @pl.when(s <= groups)
        def _():
            gradient(s - 1)

        return carry

    lax.fori_loop(1, half - 1, both, 0)

    exchanged(z)
    for h in range(2):
        total = own[z, h] + yin[z, h].astype(F32)
        for d in range(2):
            ring_arrival(d, h, 0, z).wait_recv()
            total = total + ring[d, h, 0]
        ig_ref[:, h * cols:(h + 1) * cols] = total.astype(BF16)

    total = sent[a].astype(F32)
    for k in range(1, groups):
        for g in range(4):
            dp_copy(k, g).wait_recv()
        total = total + dpin[k - 1].astype(F32)
    ow_ref[...] = total

    pair_copy().wait_send()
    for h in range(2):
        for d in range(2):
            lax.fori_loop(0, hops(h, d), lambda s, c: (gather_copy(h, d, s).wait_send(), c)[1], 0)
            lax.fori_loop(
                1, hops(h, d) + 1,
                lambda k, c: (ring_copy(d, h, k, plane(z + sign[d] * k)).wait_send(), c)[1], 0,
            )

    def drain(p, carry):
        across_copy(p).wait_send()
        exchange_copy(p).wait_send()
        return carry

    lax.fori_loop(0, planes, drain, 0)
    for k in range(1, groups):
        for g in range(4):
            dp_copy(k, g).wait_send()


def body(activations, cotangent, weight, residual, step_size, kept_blocks):
    rows, width = activations.shape
    hid = cotangent.shape[1]
    pairs = cotangent.shape[0] // (2 * rows)
    half = pairs // 2
    cols = width // 2
    groups = lax.axis_size("dp")
    vmem = pl.BlockSpec(memory_space=pltpu.VMEM)
    smem = pl.BlockSpec(memory_space=pltpu.SMEM)
    hbm = pl.BlockSpec(memory_space=pl.ANY)
    dma = pltpu.SemaphoreType.DMA
    input_grad, residual_out, owned = pl.pallas_call(
        kernel,
        out_shape=(
            jax.ShapeDtypeStruct((rows, width), BF16),
            jax.ShapeDtypeStruct((width, hid), BF16),
            jax.ShapeDtypeStruct((width, BLK), F32),
        ),
        in_specs=[smem, smem, hbm, hbm, hbm, hbm],
        out_specs=(vmem, vmem, vmem),
        scratch_shapes=[
            pltpu.VMEM((2, pairs, 2, rows, cols), BF16),
            pltpu.VMEM((pairs, 2, rows, hid), BF16),
            pltpu.VMEM((width, hid), BF16),
            pltpu.VMEM((width, hid), BF16),
            pltpu.VMEM((pairs, 2, rows, cols), F32),
            pltpu.VMEM((pairs, 2, rows, cols), BF16),
            pltpu.VMEM((pairs, 2, rows, cols), BF16),
            pltpu.VMEM((2, 2, half, rows, cols), F32),
            pltpu.VMEM((groups, width, BLK), BF16),
            pltpu.VMEM((groups - 1, width, BLK), BF16),
            dma((5,)),
            dma, dma,
            dma((2, 2, half)), dma((2, 2, half)),
            dma((pairs,)), dma((pairs,)),
            dma((pairs,)), dma((pairs,)),
            dma((2, 2, half + 1)), dma((2, 2, half + 1)),
            dma((groups - 1, 4)), dma((groups - 1, 4)),
        ],
        compiler_params=pltpu.CompilerParams(
            collective_id=0, has_side_effects=True, vmem_limit_bytes=60 * 1024 * 1024
        ),
    )(
        step_size,
        kept_blocks.reshape(-1),
        activations,
        cotangent.reshape(pairs, 2, rows, hid),
        weight,
        residual[0],
    )
    return (
        input_grad,
        residual_out[None],
        owned.reshape(1, 1, 1, width // BLK, BLK, BLK),
    )


def solution(mesh):
    return jax.shard_map(
        body,
        mesh=mesh,
        in_specs=(
            P(("dp", "tensor"), "fsdp"),
            P("dp", "tensor"),
            P("fsdp", "tensor"),
            P("dp", "fsdp", "tensor"),
            P(),
            P("dp", "fsdp", "tensor", None),
        ),
        out_specs=(
            P(("dp", "tensor"), "fsdp"),
            P("dp", "fsdp", "tensor"),
            P("dp", "fsdp", "tensor", None, None, None),
        ),
        check_vma=False,
    )
```

time: 203 us -> 88 us (0.43)
  the two profiles are of different devices: /device:TPU:1 before, /device:TPU:32 now
where the time goes in v1:
time: 88 us; the launch traced here: 87.8 us
  Pallas kernels  81.9 us (93%)
  local copies, waits for them, and re-layouts  4.59 us (5%)
  between operations  1.29 us (1%)
    pallas_call x1, Pallas kernels, body(): pl.pallas_call(kernel, out_shape=(jax.ShapeDtypeStruct((rows, width), BF1...  81.9 us
    unnamed x5, local copies, waits for them, and re-layouts  4.59 us

profile of v1, /device:TPU:32, one launch (start us, length us, event | category | flops | bytes accessed | tf_op | source)
XLA Modules:
  0.0 87.8 jit_solution(6646770692156704307)
XLA Ops:
  1.3 81.9 %shard_map.85 = (bf16[32,1024]{1,0:T(8,128)(2,1)}, bf16[1024,512]{1,0:T(8,128)(2,1)}, f32[1024,128]{1,0:T(8,128)}) custom-call(f32[1]{0:T(128)S(6)} %copy.12.step_ref, s32[8]{0:T(128)} %bitcast.9, bf16[32,1024]{1,0:T(8,128)(2,1)} %acts_ref.1, bf16[16,2,32,512]{3,2,1,0:T(8,128)(2,1)} %bitcast.5, bf16[1024,512]{1,0:T(8,128)(2,1)} %w_hbm.1, ...), custom_call_target="tpu_custom_call" | custom-call | tf_op jit(solution)/shard_map/pallas_call | solution.py:293
  83.2 1.5 %copy.13 = bf16[32,1024]{1,0:T(8,128)(2,1)} copy(bf16[32,1024]{1,0:T(8,128)(2,1)} %get-tuple-element.12) | data formatting | bytes 131072
  84.7 0.0 copy-start
  84.7 2.3 %copy.14 = bf16[1,1024,512]{2,1,0:T(8,128)(2,1)} copy(bf16[1,1024,512]{2,1,0:T(8,128)(2,1)} %bitcast.7) | data formatting | bytes 2097152
  87.0 0.0 copy-done
  87.0 0.8 copy.15
Async XLA Ops:
  84.7 2.3 %copy-start = (f32[1024,128]{1,0:T(8,128)S(1)}, f32[1024,128]{1,0:T(8,128)}, u32[]{:S(2)}) copy-start(f32[1024,128]{1,0:T(8,128)} %get-tuple-element.8) | copy-start | bytes 1572868

commit v2 on v1

v2 whole, which is shorter than its diff:
```python
import contextlib

import jax
import jax.numpy as jnp
from jax import lax
from jax.experimental import pallas as pl
from jax.experimental.pallas import tpu as pltpu
from jax.sharding import PartitionSpec as P

BLK = 128
MESH = pl.DeviceIdType.MESH
NT = (((1,), (1,)), ((), ()))
F32 = jnp.float32
BF16 = jnp.bfloat16
AHEAD = 3
scope = lambda name: contextlib.nullcontext()


def kernel(
    step_ref, kept_hbm, acts_ref, cot_hbm, w_hbm, res_hbm,
    ig_ref, ro_ref, ow_ref,
    full, cot, w, res, own, yout, yin, ring, sent, dpin, kept_ref,
    local_sem, pair_send, pair_recv, ag_send, ag_recv, ya_send, ya_recv,
    yr_send, yr_recv, rs_send, rs_recv, dp_send, dp_recv,
):
    planes = cot.shape[0]
    half = planes // 2
    rows = cot.shape[2]
    part = rows // 2
    hid = cot.shape[3]
    cols = full.shape[4]
    a = lax.axis_index("dp")
    f = lax.axis_index("fsdp")
    t = lax.axis_index("tensor")
    groups = lax.axis_size("dp")
    z = t // 2
    par = t % 2

    def plane(p):
        return lax.rem(p + 2 * planes, planes)

    up = (a, f, plane(z + 1) * 2 + par)
    down = (a, f, plane(z - 1) * 2 + par)
    pair = (a, f, z * 2 + 1 - par)
    zdev = (up, down)
    sign = (1, -1)

    def dpdev(k):
        return (lax.rem(a + k, groups), f, t)

    def remote(src, dst, send, recv, dev):
        return pltpu.make_async_remote_copy(
            src_ref=src, dst_ref=dst, send_sem=send, recv_sem=recv, device_id=dev, device_id_type=MESH
        )

    loads = [
        pltpu.make_async_copy(acts_ref.at[:, pl.ds(0, cols)], full.at[0, z, par], local_sem.at[0]),
        pltpu.make_async_copy(acts_ref.at[:, pl.ds(cols, cols)], full.at[1, z, par], local_sem.at[1]),
        pltpu.make_async_copy(cot_hbm, cot, local_sem.at[2]),
        pltpu.make_async_copy(w_hbm, w, local_sem.at[3]),
        pltpu.make_async_copy(res_hbm, res, local_sem.at[4]),
        pltpu.make_async_copy(kept_hbm, kept_ref, local_sem.at[5]),
    ]
    for load in loads:
        load.start()

    with scope("bar"):
        barrier = pltpu.get_barrier_semaphore()
        others = [up, down, pair] + [dpdev(k) for k in range(1, groups)]
        for dev in others:
            pl.semaphore_signal(barrier, inc=1, device_id=dev, device_id_type=MESH)
        pl.semaphore_wait(barrier, len(others))

    def pair_copy():
        return remote(full.at[0, z, par], full.at[0, z, par], pair_send, pair_recv, pair)

    def pair_arrival():
        return remote(full.at[0, z, 1 - par], full.at[0, z, 1 - par], pair_send, pair_recv, pair)

    chains = ((1, par), (0, par), (0, 1 - par))

    def longer(h, d):
        return lax.rem(h + d, 2)

    def hops(h, d):
        return half if h == d else half - 1

    def gather_copy(c, d, s):
        h, q = chains[c]
        ref = full.at[h, plane(z - sign[d] * s), q]
        return remote(ref, ref, ag_send.at[c, d, s], ag_recv.at[c, d, s], zdev[d])

    def gather_arrival(c, d, s):
        h, q = chains[c]
        ref = full.at[h, plane(z - sign[d] * (s + 1)), q]
        return remote(ref, ref, ag_send.at[c, d, s], ag_recv.at[c, d, s], zdev[d])

    def across_copy(p):
        ref = full.at[1, p, par]
        return remote(ref, ref, ya_send.at[p], ya_recv.at[p], pair)

    def across_arrival(p):
        ref = full.at[1, p, 1 - par]
        return remote(ref, ref, ya_send.at[p], ya_recv.at[p], pair)

    def exchange_copy(p, h):
        return remote(yout.at[p, h], yin.at[p, h], yr_send.at[p, h], yr_recv.at[p, h], pair)

    def ring_copy(d, h, i, k, p):
        lines = pl.ds(i * part, part)
        return remote(
            own.at[p, h, lines], ring.at[d, h, k - 1, lines],
            rs_send.at[d, h, i, k], rs_recv.at[d, h, i, k - 1], zdev[d],
        )

    def ring_arrival(d, h, i, k, p):
        lines = pl.ds(i * part, part)
        return remote(
            own.at[p, h, lines], ring.at[d, h, k, lines],
            rs_send.at[d, h, i, k], rs_recv.at[d, h, i, k], zdev[d],
        )

    def dp_copy(k, g):
        lines = pl.ds(pl.multiple_of(g * 2 * BLK, 2 * BLK), 2 * BLK)
        return remote(
            sent.at[lax.rem(a + k, groups), lines], dpin.at[k - 1, lines],
            dp_send.at[k - 1, g], dp_recv.at[k - 1, g], dpdev(k),
        )

    def partial(b, parity):
        x = cot[pl.ds(b * half, half), parity].reshape(half * rows, hid)
        return lax.dot_general(x, w[...], NT, preferred_element_type=F32).reshape(half, rows, 2 * cols)

    def theirs(b):
        y = partial(b, 1 - par).astype(BF16)
        yout[pl.ds(b * half, half), 0] = y[:, :, :cols]
        yout[pl.ds(b * half, half), 1] = y[:, :, cols:]

    def ours(b):
        y = partial(b, par)
        own[pl.ds(b * half, half), 0] = y[:, :, :cols]
        own[pl.ds(b * half, half), 1] = y[:, :, cols:]

    def gather_step(s):
        for c in range(3):
            for d in range(2):
                h = chains[c][0]

                def arrive():
                    gather_arrival(c, d, s).wait_recv()
                    if h == 1:
                        across_copy(plane(z - sign[d] * (s + 1))).start()

                if h == d:
                    arrive()
                else:
                    pl.when(s + 1 < half)(arrive)

                @pl.when(s + 1 < hops(h, d))
                def _():
                    gather_copy(c, d, s + 1).start()

    def exchange(r):
        h, k = r % 2, half - r // 2
        exchange_copy(plane(z + k), h).start()

        @pl.when((k > 0) & (k < half))
        def _():
            exchange_copy(plane(z - k), h).start()

    def ring_step(r):
        h, k = r % 2, half - r // 2
        for d in range(2):
            p = plane(z + sign[d] * k)

            def ring_part():
                exchange_copy(p, h).wait_recv()
                for i in range(2):
                    lines = pl.ds(i * part, part)

                    @pl.when(k < half - longer(h, d))
                    def _():
                        ring_arrival(d, h, i, k, p).wait_recv()
                        own[p, h, lines] = own[p, h, lines] + ring[d, h, k, lines]

                    own[p, h, lines] = own[p, h, lines] + yin[p, h, lines].astype(F32)
                    ring_copy(d, h, i, k, p).start()

            pl.when(k <= half - longer(h, d))(ring_part)

    def gradient(g):
        h = g // 2
        lanes = pl.ds(pl.multiple_of((g % 2) * 2 * BLK, 2 * BLK), 2 * BLK)
        lines = pl.ds(pl.multiple_of(g * 2 * BLK, 2 * BLK), 2 * BLK)
        step = step_ref[0]
        kept = [kept_ref[i] for i in range(kept_ref.shape[0])]
        x = full[h, :, :, :, lanes].reshape(planes * 2 * rows, 2 * BLK)
        y = cot[...].reshape(planes * 2 * rows, hid)
        grad = lax.dot_general(x, y, (((0,), (0,)), ((), ())), preferred_element_type=F32)
        rounded = (res[lines].astype(F32) + step * grad).astype(BF16)
        for i in range(2):
            for o in range(groups):
                number = (2 * g + i) * groups + o
                hit = kept[0] == number
                for other in kept[1:]:
                    hit = jnp.logical_or(hit, other == number)
                keep = jnp.where(hit, 1.0, 0.0)
                block = rounded[i * BLK:(i + 1) * BLK, o * BLK:(o + 1) * BLK].astype(F32)
                here = pl.ds(pl.multiple_of((2 * g + i) * BLK, BLK), BLK)
                ro_ref[here, o * BLK:(o + 1) * BLK] = (block * (1.0 - keep)).astype(BF16)
                sent[o, here] = (block * keep).astype(BF16)
        for k in range(1, groups):
            dp_copy(k, g).start()

    def loop(first, last, f):
        lax.fori_loop(first, last, lambda i, c: (f(i), c)[1], 0)

    with scope("ld0"):
        loads[0].wait()
        loads[1].wait()
    pair_copy().start()
    for c in range(2):
        for d in range(2):
            gather_copy(c, d, 0).start()
    across_copy(z).start()
    with scope("ld2"):
        loads[2].wait()
        loads[3].wait()
    with scope("theirs"):
        loop(0, 2, theirs)
    with scope("pair"):
        pair_arrival().wait_recv()
        for d in range(2):
            gather_copy(2, d, 0).start()
    loop(0, AHEAD, exchange)
    with scope("ours"):
        loop(0, 2, ours)

    def slot(s):
        @pl.when(s < half)
        def _():
            with scope("ag"):
                gather_step(s)

        @pl.when(s + AHEAD < planes + 2)
        def _():
            exchange(s + AHEAD)

        with scope("rs"):
            ring_step(s)

        @pl.when(s == half - 1)
        def _():
            with scope("across"):
                loop(0, planes, lambda p: across_arrival(p).wait_recv())
                for load in loads[4:]:
                    load.wait()

        @pl.when((s >= half - 1) & (s < half + 3))
        def _():
            with scope("grad"):
                gradient(s - half + 1)

    loop(0, planes, slot)

    with scope("rs_last"):
        for h in range(2):
            exchange_copy(z, h).wait_recv()
            for i in range(2):
                lines = pl.ds(i * part, part)
                total = own[z, h, lines] + yin[z, h, lines].astype(F32)
                for d in range(2):
                    ring_arrival(d, h, i, 0, z).wait_recv()
                    total = total + ring[d, h, 0, lines]
                ig_ref[lines, h * cols:(h + 1) * cols] = total.astype(BF16)

    with scope("dpsum"):
        total = sent[a].astype(F32)
        for k in range(1, groups):
            for g in range(4):
                dp_copy(k, g).wait_recv()
            total = total + dpin[k - 1].astype(F32)
        ow_ref[...] = total

    with scope("drain"):
        pair_copy().wait_send()
        for d in range(2):
            for c in range(3):
                loop(0, hops(chains[c][0], d), lambda s: gather_copy(c, d, s).wait_send())
            for h in range(2):
                for i in range(2):
                    loop(
                        1, hops(h, d) + 1,
                        lambda k: ring_copy(d, h, i, k, plane(z + sign[d] * k)).wait_send(),
                    )

        def left(p):
            across_copy(p).wait_send()
            for h in range(2):
                exchange_copy(p, h).wait_send()

        loop(0, planes, left)
        for k in range(1, groups):
            for g in range(4):
                dp_copy(k, g).wait_send()


def place(ig_in, ro_in, ow_in, ig_out, ro_out, ow_out, sem):
    copies = [
        pltpu.make_async_copy(src, dst, sem.at[i])
        for i, (src, dst) in enumerate(((ro_in, ro_out), (ow_in, ow_out), (ig_in, ig_out)))
    ]
    for copy in copies:
        copy.start()
    for copy in copies:
        copy.wait()


def body(activations, cotangent, weight, residual, step_size, kept_blocks):
    rows, width = activations.shape
    hid = cotangent.shape[1]
    pairs = cotangent.shape[0] // (2 * rows)
    half = pairs // 2
    cols = width // 2
    groups = lax.axis_size("dp")
    vmem = pl.BlockSpec(memory_space=pltpu.VMEM)
    smem = pl.BlockSpec(memory_space=pltpu.SMEM)
    hbm = pl.BlockSpec(memory_space=pltpu.HBM)
    dma = pltpu.SemaphoreType.DMA
    results = pl.pallas_call(
        kernel,
        out_shape=(
            pltpu.VMEM((rows, width), BF16),
            pltpu.VMEM((width, hid), BF16),
            pltpu.VMEM((width, BLK), F32),
        ),
        in_specs=[smem] + [hbm] * 5,
        out_specs=(vmem, vmem, vmem),
        scratch_shapes=[
            pltpu.VMEM((2, pairs, 2, rows, cols), BF16),
            pltpu.VMEM((pairs, 2, rows, hid), BF16),
            pltpu.VMEM((width, hid), BF16),
            pltpu.VMEM((width, hid), BF16),
            pltpu.VMEM((pairs, 2, rows, cols), F32),
            pltpu.VMEM((pairs, 2, rows, cols), BF16),
            pltpu.VMEM((pairs, 2, rows, cols), BF16),
            pltpu.VMEM((2, 2, half, rows, cols), F32),
            pltpu.VMEM((groups, width, BLK), BF16),
            pltpu.VMEM((groups - 1, width, BLK), BF16),
            pltpu.SMEM(kept_blocks.shape[-1:], jnp.int32),
            dma((6,)),
            dma, dma,
            dma((3, 2, half)), dma((3, 2, half)),
            dma((pairs,)), dma((pairs,)),
            dma((pairs, 2)), dma((pairs, 2)),
            dma((2, 2, 2, half + 1)), dma((2, 2, 2, half + 1)),
            dma((groups - 1, 4)), dma((groups - 1, 4)),
        ],
        compiler_params=pltpu.CompilerParams(
            collective_id=0, has_side_effects=True, vmem_limit_bytes=48 * 1024 * 1024
        ),
    )(
        step_size,
        *[pltpu.with_memory_space_constraint(x, pltpu.HBM) for x in (
            kept_blocks.reshape(-1),
            activations,
            cotangent.reshape(pairs, 2, rows, hid),
            weight,
            residual[0],
        )]
    )
    input_grad, residual_out, owned = pl.pallas_call(
        place,
        out_shape=tuple(jax.ShapeDtypeStruct(x.shape, x.dtype) for x in results),
        in_specs=[vmem] * 3,
        out_specs=(hbm, hbm, hbm),
        scratch_shapes=[dma((3,))],
    )(*[pltpu.with_memory_space_constraint(x, pltpu.VMEM) for x in results])
    return (
        input_grad,
        residual_out[None],
        owned.reshape(1, 1, 1, width // BLK, BLK, BLK),
    )


def solution(mesh):
    return jax.shard_map(
        body,
        mesh=mesh,
        in_specs=(
            P(("dp", "tensor"), "fsdp"),
            P("dp", "tensor"),
            P("fsdp", "tensor"),
            P("dp", "fsdp", "tensor"),
            P(),
            P("dp", "fsdp", "tensor", None),
        ),
        out_specs=(
            P(("dp", "tensor"), "fsdp"),
            P("dp", "fsdp", "tensor"),
            P("dp", "fsdp", "tensor", None, None, None),
        ),
        check_vma=False,
    )
```

time: 88 us -> 67.4 us (0.77)
  the two profiles are of different devices: /device:TPU:32 before, /device:TPU:16 now
where the time goes in v2:
time: 67.4 us; the launch traced here: 67.3 us
  Pallas kernels  66 us (98%)
  between operations  1.29 us (2%)
    pallas_call x1, Pallas kernels, body(): pl.pallas_call(kernel, out_shape=(pltpu.VMEM((rows, width), BF16), pltpu....  64.8 us

profile of v2, /device:TPU:16, one launch (start us, length us, event | category | flops | bytes accessed | tf_op | source)
XLA Modules:
  0.0 67.3 jit_solution(18168388166891090688)
XLA Ops:
  1.3 64.8 %shard_map.85 = (bf16[32,1024]{1,0:T(8,128)(2,1)S(1)}, bf16[1024,512]{1,0:T(8,128)(2,1)S(1)}, f32[1024,128]{1,0:T(8,128)S(1)}) custom-call(f32[1]{0:T(128)S(6)} %copy.9.step_ref, s32[8]{0:T(128)} %bitcast.7, bf16[32,1024]{1,0:T(8,128)(2,1)} %acts_ref.1, bf16[16,2,32,512]{3,2,1,0:T(8,128)(2,1)} %bitcast.5, bf16[1024,512]{1,0:T(8,128)(2,1)} %w_hbm.1, ...), custom_call_target="tpu_custom_call" | custom-call | tf_op jit(solution)/shard_map/pallas_call | solution.py:330
  66.1 1.2 %shard_map.86 = (bf16[32,1024]{1,0:T(8,128)(2,1)}, bf16[1024,512]{1,0:T(8,128)(2,1)}, f32[1024,128]{1,0:T(8,128)}) custom-call(bf16[32,1024]{1,0:T(8,128)(2,1)S(1)} %get-tuple-element.9.ig_in, bf16[1024,512]{1,0:T(8,128)(2,1)S(1)} %get-tuple-element.10.ro_in, f32[1024,128]{1,0:T(8,128)S(1)} %get-tuple-element.11.ow_in), custom_call_target="tpu_custom_call" | custom-call | tf_op jit(solution)/shard_map/pallas_call | solution.py:372

commit v3 on v2

v3 whole, which is shorter than its diff:
```python
import contextlib

import jax
import jax.numpy as jnp
from jax import lax
from jax.experimental import pallas as pl
from jax.experimental.pallas import tpu as pltpu
from jax.sharding import PartitionSpec as P

BLK = 128
MESH = pl.DeviceIdType.MESH
NT = (((1,), (1,)), ((), ()))
F32 = jnp.float32
BF16 = jnp.bfloat16
scope = lambda name: contextlib.nullcontext()


def kernel(
    step_ref, kept_hbm, acts_ref, cot_hbm, w_hbm, res_hbm,
    ig_ref, ro_ref, ow_ref,
    full, cot, w, res, own, yout, yin, early, ring16, ring, sent, dpin, kept_ref,
    local_sem, pair_send, pair_recv, ag_send, ag_recv, ya_send, ya_recv,
    yr_send, yr_recv, re_send, re_recv, rs_send, rs_recv, dp_send, dp_recv,
):
    planes = cot.shape[0]
    half = planes // 2
    rows = cot.shape[2]
    part = rows // 2
    hid = cot.shape[3]
    cols = full.shape[4]
    a = lax.axis_index("dp")
    f = lax.axis_index("fsdp")
    t = lax.axis_index("tensor")
    groups = lax.axis_size("dp")
    z = t // 2
    par = t % 2

    def plane(p):
        return lax.rem(p + 2 * planes, planes)

    pair = (a, f, z * 2 + 1 - par)
    sign = (1, -1)
    zdev = [(a, f, plane(z + v) * 2 + par) for v in sign]
    zpair = [(a, f, plane(z + v) * 2 + 1 - par) for v in sign]

    def dpdev(k):
        return (lax.rem(a + k, groups), f, t)

    def remote(src, dst, send, recv, dev):
        return pltpu.make_async_remote_copy(
            src_ref=src, dst_ref=dst, send_sem=send, recv_sem=recv, device_id=dev, device_id_type=MESH
        )

    def take(ref, sem):
        pltpu.make_async_copy(ref, ref, sem).wait()

    def loop(first, last, f):
        lax.fori_loop(first, last, lambda i, c: (f(i), c)[1], 0)

    loads = [
        pltpu.make_async_copy(acts_ref.at[:, pl.ds(0, cols)], full.at[0, z, par], local_sem.at[0]),
        pltpu.make_async_copy(acts_ref.at[:, pl.ds(cols, cols)], full.at[1, z, par], local_sem.at[1]),
        pltpu.make_async_copy(cot_hbm, cot, local_sem.at[2]),
        pltpu.make_async_copy(w_hbm, w, local_sem.at[3]),
        pltpu.make_async_copy(res_hbm, res, local_sem.at[4]),
        pltpu.make_async_copy(kept_hbm, kept_ref, local_sem.at[5]),
    ]
    for load in loads:
        load.start()

    with scope("bar"):
        barrier = pltpu.get_barrier_semaphore()
        others = zdev + zpair + [pair] + [dpdev(k) for k in range(1, groups)]
        for dev in others:
            pl.semaphore_signal(barrier, inc=1, device_id=dev, device_id_type=MESH)
        pl.semaphore_wait(barrier, len(others))

    chains = ((1, par), (0, par), (0, 1 - par))

    def shorter(h, d):
        return lax.rem(h + d, 2)

    def hops(h, d):
        return half if h == d else half - 1

    def gather_copy(c, d, s):
        h, q = chains[c]
        ref = full.at[h, plane(z - sign[d] * s), q]
        return remote(ref, ref, ag_send.at[c], ag_recv.at[c, d, s], zdev[d])

    def gather_first(c, d):
        h = chains[c][0]
        ref = full.at[h, z, par]
        return remote(ref, ref, ag_send.at[c], ag_recv.at[c, d, 0], zpair[d] if c == 2 else zdev[d])

    def gather_arrival(c, d, s):
        h, q = chains[c]
        take(full.at[h, plane(z - sign[d] * (s + 1)), q], ag_recv.at[c, d, s])

    def across_copy(p):
        ref = full.at[1, p, par]
        return remote(ref, ref, ya_send, ya_recv, pair)

    def gather_step(s):
        for c in range(3):
            for d in range(2):
                h = chains[c][0]

                def arrive():
                    gather_arrival(c, d, s)
                    if h == 1:
                        across_copy(plane(z - sign[d] * (s + 1))).start()

                if h == d:
                    arrive()
                else:
                    pl.when(s + 1 < half)(arrive)

                @pl.when(s + 1 < hops(h, d))
                def _():
                    gather_copy(c, d, s + 1).start()

    def exchange(r):
        h, k = r % 2, half - r // 2

        def send(p):
            remote(yout.at[p, h], yin.at[p, h], yr_send, yr_recv.at[h, k], pair).start()

        send(plane(z + k))

        @pl.when((k > 0) & (k < half))
        def _():
            send(plane(z - k))

    def exchanged(h, k, n):
        take(yin.at[pl.ds(0, n), 0], yr_recv.at[h, k])

    def early_step(s):
        for h in range(2):
            @pl.when(s == 0)
            def _():
                exchanged(h, half, 1)

            @pl.when(s == 1)
            def _():
                exchanged(h, half - 1, 2)

            for d in range(2):
                p = plane(z + sign[d] * (half - s))

                def pass_on():
                    total = own[p, h] + yin[p, h].astype(F32)
                    early[d, h, s] = total.astype(BF16)
                    remote(
                        early.at[d, h, s], ring16.at[d, h, s],
                        re_send, re_recv.at[d, h, s], zdev[d],
                    ).start()

                if h == d:
                    @pl.when(s == 1)
                    def _():
                        take(ring16.at[d, h, 0], re_recv.at[d, h, 0])
                        own[p, h] = own[p, h] + ring16[d, h, 0].astype(F32)

                    pass_on()
                else:
                    pl.when(s == 1)(pass_on)

    def ring_step(r):
        h, k = r % 2, half - r // 2
        exchanged(h, k, 2)
        for d in range(2):
            p = plane(z + sign[d] * k)

            @pl.when(k == half - 2)
            def _():
                take(ring16.at[d, h, 1], re_recv.at[d, h, 1])
                own[p, h] = own[p, h] + ring16[d, h, 1].astype(F32)

            for i in range(2):
                lines = pl.ds(i * part, part)

                @pl.when(k < half - 2)
                def _():
                    take(ring.at[d, h, k, lines], rs_recv.at[d, h, k, i])
                    own[p, h, lines] = own[p, h, lines] + ring[d, h, k, lines]

                own[p, h, lines] = own[p, h, lines] + yin[p, h, lines].astype(F32)
                remote(
                    own.at[p, h, lines], ring.at[d, h, k - 1, lines],
                    rs_send, rs_recv.at[d, h, k - 1, i], zdev[d],
                ).start()

    def partial(b, parity):
        x = cot[pl.ds(b * half, half), parity].reshape(half * rows, hid)
        return lax.dot_general(x, w[...], NT, preferred_element_type=F32).reshape(half, rows, 2 * cols)

    def theirs(b):
        y = partial(b, 1 - par).astype(BF16)
        yout[pl.ds(b * half, half), 0] = y[:, :, :cols]
        yout[pl.ds(b * half, half), 1] = y[:, :, cols:]

    def ours(b):
        y = partial(b, par)
        own[pl.ds(b * half, half), 0] = y[:, :, :cols]
        own[pl.ds(b * half, half), 1] = y[:, :, cols:]

    def gradient(g):
        h = g // 2
        lanes = pl.ds(pl.multiple_of((g % 2) * 2 * BLK, 2 * BLK), 2 * BLK)
        lines = pl.ds(pl.multiple_of(g * 2 * BLK, 2 * BLK), 2 * BLK)
        step = step_ref[0]
        kept = [kept_ref[i] for i in range(kept_ref.shape[0])]
        x = full[h, :, :, :, lanes].reshape(planes * 2 * rows, 2 * BLK)
        y = cot[...].reshape(planes * 2 * rows, hid)
        grad = lax.dot_general(x, y, (((0,), (0,)), ((), ())), preferred_element_type=F32)
        rounded = (res[lines].astype(F32) + step * grad).astype(BF16)
        for i in range(2):
            for o in range(groups):
                number = (2 * g + i) * groups + o
                hit = kept[0] == number
                for other in kept[1:]:
                    hit = jnp.logical_or(hit, other == number)
                keep = jnp.where(hit, 1.0, 0.0)
                block = rounded[i * BLK:(i + 1) * BLK, o * BLK:(o + 1) * BLK].astype(F32)
                here = pl.ds(pl.multiple_of((2 * g + i) * BLK, BLK), BLK)
                ro_ref[here, o * BLK:(o + 1) * BLK] = (block * (1.0 - keep)).astype(BF16)
                sent[o, here] = (block * keep).astype(BF16)
        for k in range(1, groups):
            remote(
                sent.at[lax.rem(a + k, groups), lines], dpin.at[k - 1, lines], dp_send, dp_recv, dpdev(k)
            ).start()

    with scope("ld0"):
        loads[0].wait()
        loads[1].wait()
    for c in range(3):
        for d in range(2):
            gather_first(c, d).start()
    pair_copy = remote(full.at[0, z, par], full.at[0, z, par], pair_send, pair_recv, pair)
    pair_copy.start()
    across_copy(z).start()
    with scope("ld2"):
        loads[2].wait()
        loads[3].wait()
    with scope("theirs"):
        loop(0, 2, theirs)
    loop(0, 4, exchange)
    with scope("ours"):
        loop(0, 2, ours)

    def slot(s):
        @pl.when(s < half)
        def _():
            with scope("ag"):
                gather_step(s)

        @pl.when(s + 4 < planes + 2)
        def _():
            exchange(s + 4)

        @pl.when(s < 2)
        def _():
            with scope("early"):
                early_step(s)

        @pl.when(s >= 2)
        def _():
            with scope("rs"):
                ring_step(s + 2)

        @pl.when(s == half - 1)
        def _():
            take(full.at[0, z, 1 - par], pair_recv)
            for load in loads[4:]:
                load.wait()

        @pl.when(s == half + 1)
        def _():
            with scope("across"):
                take(full.at[1, :, 1 - par], ya_recv)

        @pl.when((s >= half - 1) & (s < half + 3))
        def _():
            with scope("grad"):
                gradient(s - half + 1)

    loop(0, planes - 2, slot)

    with scope("rs_last"):
        for h in range(2):
            exchanged(h, 0, 1)
            for i in range(2):
                lines = pl.ds(i * part, part)
                total = own[z, h, lines] + yin[z, h, lines].astype(F32)
                for d in range(2):
                    take(ring.at[d, h, 0, lines], rs_recv.at[d, h, 0, i])
                    total = total + ring[d, h, 0, lines]
                ig_ref[lines, h * cols:(h + 1) * cols] = total.astype(BF16)

    with scope("dpsum"):
        take(dpin, dp_recv)
        total = sent[a].astype(F32)
        for k in range(1, groups):
            total = total + dpin[k - 1].astype(F32)
        ow_ref[...] = total

    with scope("drain"):
        pair_copy.wait_send()
        for c in range(3):
            take(full.at[0, pl.ds(0, planes - 1), 0], ag_send.at[c])
        take(full.at[0, :, 0], ya_send)
        take(yout, yr_send)
        take(yout.at[pl.ds(0, 3)], re_send)
        take(own.at[pl.ds(0, 2 * (half - 2))], rs_send)
        take(dpin, dp_send)


def place(ig_in, ro_in, ow_in, ig_out, ro_out, ow_out, sem):
    copies = [
        pltpu.make_async_copy(src, dst, sem.at[i])
        for i, (src, dst) in enumerate(((ro_in, ro_out), (ow_in, ow_out), (ig_in, ig_out)))
    ]
    for copy in copies:
        copy.start()
    for copy in copies:
        copy.wait()


def body(activations, cotangent, weight, residual, step_size, kept_blocks):
    rows, width = activations.shape
    hid = cotangent.shape[1]
    pairs = cotangent.shape[0] // (2 * rows)
    half = pairs // 2
    cols = width // 2
    groups = lax.axis_size("dp")
    vmem = pl.BlockSpec(memory_space=pltpu.VMEM)
    smem = pl.BlockSpec(memory_space=pltpu.SMEM)
    hbm = pl.BlockSpec(memory_space=pltpu.HBM)
    dma = pltpu.SemaphoreType.DMA
    results = pl.pallas_call(
        kernel,
        out_shape=(
            pltpu.VMEM((rows, width), BF16),
            pltpu.VMEM((width, hid), BF16),
            pltpu.VMEM((width, BLK), F32),
        ),
        in_specs=[smem] + [hbm] * 5,
        out_specs=(vmem, vmem, vmem),
        scratch_shapes=[
            pltpu.VMEM((2, pairs, 2, rows, cols), BF16),
            pltpu.VMEM((pairs, 2, rows, hid), BF16),
            pltpu.VMEM((width, hid), BF16),
            pltpu.VMEM((width, hid), BF16),
            pltpu.VMEM((pairs, 2, rows, cols), F32),
            pltpu.VMEM((pairs, 2, rows, cols), BF16),
            pltpu.VMEM((pairs, 2, rows, cols), BF16),
            pltpu.VMEM((2, 2, 2, rows, cols), BF16),
            pltpu.VMEM((2, 2, 2, rows, cols), BF16),
            pltpu.VMEM((2, 2, half - 2, rows, cols), F32),
            pltpu.VMEM((groups, width, BLK), BF16),
            pltpu.VMEM((groups - 1, width, BLK), BF16),
            pltpu.SMEM(kept_blocks.shape[-1:], jnp.int32),
            dma((6,)),
            dma, dma,
            dma((3,)), dma((3, 2, half)),
            dma, dma,
            dma, dma((2, half + 1)),
            dma, dma((2, 2, 2)),
            dma, dma((2, 2, half - 2, 2)),
            dma, dma,
        ],
        compiler_params=pltpu.CompilerParams(
            collective_id=0, has_side_effects=True, vmem_limit_bytes=48 * 1024 * 1024
        ),
    )(
        step_size,
        *[pltpu.with_memory_space_constraint(x, pltpu.HBM) for x in (
            kept_blocks.reshape(-1),
            activations,
            cotangent.reshape(pairs, 2, rows, hid),
            weight,
            residual[0],
        )]
    )
    input_grad, residual_out, owned = pl.pallas_call(
        place,
        out_shape=tuple(jax.ShapeDtypeStruct(x.shape, x.dtype) for x in results),
        in_specs=[vmem] * 3,
        out_specs=(hbm, hbm, hbm),
        scratch_shapes=[dma((3,))],
    )(*[pltpu.with_memory_space_constraint(x, pltpu.VMEM) for x in results])
    return (
        input_grad,
        residual_out[None],
        owned.reshape(1, 1, 1, width // BLK, BLK, BLK),
    )


def solution(mesh):
    return jax.shard_map(
        body,
        mesh=mesh,
        in_specs=(
            P(("dp", "tensor"), "fsdp"),
            P("dp", "tensor"),
            P("fsdp", "tensor"),
            P("dp", "fsdp", "tensor"),
            P(),
            P("dp", "fsdp", "tensor", None),
        ),
        out_specs=(
            P(("dp", "tensor"), "fsdp"),
            P("dp", "fsdp", "tensor"),
            P("dp", "fsdp", "tensor", None, None, None),
        ),
        check_vma=False,
    )
```

time: 67.4 us -> 59.6 us (0.88)
  Pallas kernels: 66 us -> 58.2 us
    pallas_call x1, Pallas kernels: 64.8 us -> 57 us  [body(): pl.pallas_call(kernel, out_shape=(pltpu.VMEM((rows, width), BF16), pltpu....]
where the time goes in v3:
time: 59.6 us; the launch traced here: 59.5 us
  Pallas kernels  58.2 us (98%)
  between operations  1.29 us (2%)
    pallas_call x1, Pallas kernels, body(): pl.pallas_call(kernel, out_shape=(pltpu.VMEM((rows, width), BF16), pltpu....  57 us

profile of v3, /device:TPU:16, one launch (start us, length us, event | category | flops | bytes accessed | tf_op | source)
XLA Modules:
  0.0 59.5 jit_solution(3756253865262482130)
XLA Ops:
  1.3 57.0 %shard_map.85 = (bf16[32,1024]{1,0:T(8,128)(2,1)S(1)}, bf16[1024,512]{1,0:T(8,128)(2,1)S(1)}, f32[1024,128]{1,0:T(8,128)S(1)}) custom-call(f32[1]{0:T(128)S(6)} %copy.9.step_ref, s32[8]{0:T(128)} %bitcast.7, bf16[32,1024]{1,0:T(8,128)(2,1)} %acts_ref.1, bf16[16,2,32,512]{3,2,1,0:T(8,128)(2,1)} %bitcast.5, bf16[1024,512]{1,0:T(8,128)(2,1)} %w_hbm.1, ...), custom_call_target="tpu_custom_call" | custom-call | tf_op jit(solution)/shard_map/pallas_call | solution.py:341
  58.3 1.2 %shard_map.86 = (bf16[32,1024]{1,0:T(8,128)(2,1)}, bf16[1024,512]{1,0:T(8,128)(2,1)}, f32[1024,128]{1,0:T(8,128)}) custom-call(bf16[32,1024]{1,0:T(8,128)(2,1)S(1)} %get-tuple-element.9.ig_in, bf16[1024,512]{1,0:T(8,128)(2,1)S(1)} %get-tuple-element.10.ro_in, f32[1024,128]{1,0:T(8,128)S(1)} %get-tuple-element.11.ow_in), custom_call_target="tpu_custom_call" | custom-call | tf_op jit(solution)/shard_map/pallas_call | solution.py:386

commit v4 on v3

--- a/solution.py
+++ b/solution.py
@@ -12,6 +12,7 @@
 NT = (((1,), (1,)), ((), ()))
 F32 = jnp.float32
 BF16 = jnp.bfloat16
+AHEAD = 2
 scope = lambda name: contextlib.nullcontext()
 
 
@@ -57,6 +58,11 @@
     def loop(first, last, f):
         lax.fori_loop(first, last, lambda i, c: (f(i), c)[1], 0)
 
+    barrier = pltpu.get_barrier_semaphore()
+    others = zdev + zpair + [pair] + [dpdev(k) for k in range(1, groups)]
+    for dev in others:
+        pl.semaphore_signal(barrier, inc=1, device_id=dev, device_id_type=MESH)
+
     loads = [
         pltpu.make_async_copy(acts_ref.at[:, pl.ds(0, cols)], full.at[0, z, par], local_sem.at[0]),
         pltpu.make_async_copy(acts_ref.at[:, pl.ds(cols, cols)], full.at[1, z, par], local_sem.at[1]),
@@ -69,10 +75,6 @@
         load.start()
 
     with scope("bar"):
-        barrier = pltpu.get_barrier_semaphore()
-        others = zdev + zpair + [pair] + [dpdev(k) for k in range(1, groups)]
-        for dev in others:
-            pl.semaphore_signal(barrier, inc=1, device_id=dev, device_id_type=MESH)
         pl.semaphore_wait(barrier, len(others))
 
     chains = ((1, par), (0, par), (0, 1 - par))
@@ -191,19 +193,24 @@
                     rs_send, rs_recv.at[d, h, k - 1, i], zdev[d],
                 ).start()
 
+    def planes_of(b):
+        return [plane(z + half // 2 + half * b + i) for i in range(half)]
+
     def partial(b, parity):
-        x = cot[pl.ds(b * half, half), parity].reshape(half * rows, hid)
-        return lax.dot_general(x, w[...], NT, preferred_element_type=F32).reshape(half, rows, 2 * cols)
+        x = jnp.concatenate([cot[p, parity] for p in planes_of(b)], axis=0)
+        return lax.dot_general(x, w[...], NT, preferred_element_type=F32)
 
     def theirs(b):
         y = partial(b, 1 - par).astype(BF16)
-        yout[pl.ds(b * half, half), 0] = y[:, :, :cols]
-        yout[pl.ds(b * half, half), 1] = y[:, :, cols:]
+        for i, p in enumerate(planes_of(b)):
+            for h in range(2):
+                yout[p, h] = y[i * rows:(i + 1) * rows, h * cols:(h + 1) * cols]
 
     def ours(b):
         y = partial(b, par)
-        own[pl.ds(b * half, half), 0] = y[:, :, :cols]
-        own[pl.ds(b * half, half), 1] = y[:, :, cols:]
+        for i, p in enumerate(planes_of(b)):
+            for h in range(2):
+                own[p, h] = y[i * rows:(i + 1) * rows, h * cols:(h + 1) * cols]
 
     def gradient(g):
         h = g // 2
@@ -231,6 +238,11 @@
                 sent.at[lax.rem(a + k, groups), lines], dpin.at[k - 1, lines], dp_send, dp_recv, dpdev(k)
             ).start()
 
+    share = 4 - 2 * lax.rem(f, 2)
+
+    def done(s):
+        return 1 + (s * share + 9 - 2 * share) // 3
+
     with scope("ld0"):
         loads[0].wait()
         loads[1].wait()
@@ -238,26 +250,24 @@
         for d in range(2):
             gather_first(c, d).start()
     pair_copy = remote(full.at[0, z, par], full.at[0, z, par], pair_send, pair_recv, pair)
-    pair_copy.start()
-    across_copy(z).start()
     with scope("ld2"):
         loads[2].wait()
         loads[3].wait()
     with scope("theirs"):
-        loop(0, 2, theirs)
-    loop(0, 4, exchange)
+        theirs(0)
+    loop(0, done(0) + AHEAD, exchange)
+    pair_copy.start()
+    across_copy(z).start()
     with scope("ours"):
-        loop(0, 2, ours)
+        theirs(1)
+        ours(0)
+        ours(1)
 
     def slot(s):
-        @pl.when(s < half)
-        def _():
-            with scope("ag"):
-                gather_step(s)
-
-        @pl.when(s + 4 < planes + 2)
-        def _():
-            exchange(s + 4)
+        loop(done(s) + AHEAD, done(s + 1) + AHEAD, exchange)
+
+        with scope("ag"):
+            gather_step(s)
 
         @pl.when(s < 2)
         def _():
@@ -267,25 +277,32 @@
         @pl.when(s >= 2)
         def _():
             with scope("rs"):
-                ring_step(s + 2)
-
-        @pl.when(s == half - 1)
-        def _():
-            take(full.at[0, z, 1 - par], pair_recv)
-            for load in loads[4:]:
-                load.wait()
-
-        @pl.when(s == half + 1)
+                loop(done(s), done(s + 1), ring_step)
+
+    loop(0, half, slot)
+    last = done(half)
+    loop(last + AHEAD, planes + 2, exchange)
+    take(full.at[0, z, 1 - par], pair_recv)
+    for load in loads[4:]:
+        load.wait()
+
+    def after(g):
+        @pl.when(g > 0)
+        def _():
+            with scope("rs"):
+                ring_step(last - 1 + g)
+
+        @pl.when(g == 1)
         def _():
             with scope("across"):
                 take(full.at[1, :, 1 - par], ya_recv)
 
-        @pl.when((s >= half - 1) & (s < half + 3))
+        @pl.when(g < 3)
         def _():
             with scope("grad"):
-                gradient(s - half + 1)
-
-    loop(0, planes - 2, slot)
+                loop((3 * g + 1) // 2, g + 2, gradient)
+
+    loop(0, planes - last + 1, after)
 
     with scope("rs_last"):
         for h in range(2):

time: 59.6 us -> 57.8 us (0.970)
  Pallas kernels: 58.2 us -> 56.4 us
    pallas_call x1, Pallas kernels: 57 us -> 55.2 us  [body(): pl.pallas_call(kernel, out_shape=(pltpu.VMEM((rows, width), BF16), pltpu....]
where the time goes in v4:
time: 57.8 us; the launch traced here: 57.6 us
  Pallas kernels  56.4 us (98%)
  between operations  1.29 us (2%)
    pallas_call x1, Pallas kernels, body(): pl.pallas_call(kernel, out_shape=(pltpu.VMEM((rows, width), BF16), pltpu....  55.2 us
    pallas_call x1, Pallas kernels, body(): pl.pallas_call(place, out_shape=tuple((jax.ShapeDtypeStruct(x.shape, x.dt...  1.18 us

profile of v4, /device:TPU:16, one launch (start us, length us, event | category | flops | bytes accessed | tf_op | source)
XLA Modules:
  0.0 57.6 jit_solution(2341261689171269674)
XLA Ops:
  1.3 55.2 %shard_map.85 = (bf16[32,1024]{1,0:T(8,128)(2,1)S(1)}, bf16[1024,512]{1,0:T(8,128)(2,1)S(1)}, f32[1024,128]{1,0:T(8,128)S(1)}) custom-call(f32[1]{0:T(128)S(6)} %copy.9.step_ref, s32[8]{0:T(128)} %bitcast.7, bf16[32,1024]{1,0:T(8,128)(2,1)} %acts_ref.1, bf16[16,2,32,512]{3,2,1,0:T(8,128)(2,1)} %bitcast.5, bf16[1024,512]{1,0:T(8,128)(2,1)} %w_hbm.1, ...), custom_call_target="tpu_custom_call" | custom-call | tf_op jit(solution)/shard_map/pallas_call | solution.py:358
  56.5 1.2 %shard_map.86 = (bf16[32,1024]{1,0:T(8,128)(2,1)}, bf16[1024,512]{1,0:T(8,128)(2,1)}, f32[1024,128]{1,0:T(8,128)}) custom-call(bf16[32,1024]{1,0:T(8,128)(2,1)S(1)} %get-tuple-element.9.ig_in, bf16[1024,512]{1,0:T(8,128)(2,1)S(1)} %get-tuple-element.10.ro_in, f32[1024,128]{1,0:T(8,128)S(1)} %get-tuple-element.11.ow_in), custom_call_target="tpu_custom_call" | custom-call | tf_op jit(solution)/shard_map/pallas_call | solution.py:403

commit v5 on v4

--- a/solution.py
+++ b/solution.py
@@ -88,7 +88,7 @@
     def gather_copy(c, d, s):
         h, q = chains[c]
         ref = full.at[h, plane(z - sign[d] * s), q]
-        return remote(ref, ref, ag_send.at[c], ag_recv.at[c, d, s], zdev[d])
+        return remote(ref, ref, ag_send.at[c], ag_recv.at[c, d, lax.rem(s, 3)], zdev[d])
 
     def gather_first(c, d):
         h = chains[c][0]
@@ -97,7 +97,7 @@
 
     def gather_arrival(c, d, s):
         h, q = chains[c]
-        take(full.at[h, plane(z - sign[d] * (s + 1)), q], ag_recv.at[c, d, s])
+        take(full.at[h, plane(z - sign[d] * (s + 1)), q], ag_recv.at[c, d, lax.rem(s, 3)])
 
     def across_copy(p):
         ref = full.at[1, p, par]
@@ -184,13 +184,13 @@
 
                 @pl.when(k < half - 2)
                 def _():
-                    take(ring.at[d, h, k, lines], rs_recv.at[d, h, k, i])
+                    take(ring.at[d, h, k, lines], rs_recv.at[d, h, lax.rem(k, 3), i])
                     own[p, h, lines] = own[p, h, lines] + ring[d, h, k, lines]
 
                 own[p, h, lines] = own[p, h, lines] + yin[p, h, lines].astype(F32)
                 remote(
                     own.at[p, h, lines], ring.at[d, h, k - 1, lines],
-                    rs_send, rs_recv.at[d, h, k - 1, i], zdev[d],
+                    rs_send, rs_recv.at[d, h, lax.rem(k - 1, 3), i], zdev[d],
                 ).start()
 
     def planes_of(b):
@@ -233,15 +233,15 @@
                 here = pl.ds(pl.multiple_of((2 * g + i) * BLK, BLK), BLK)
                 ro_ref[here, o * BLK:(o + 1) * BLK] = (block * (1.0 - keep)).astype(BF16)
                 sent[o, here] = (block * keep).astype(BF16)
-        for k in range(1, groups):
+        for k in (2, 1, 3):
             remote(
                 sent.at[lax.rem(a + k, groups), lines], dpin.at[k - 1, lines], dp_send, dp_recv, dpdev(k)
             ).start()
 
-    share = 4 - 2 * lax.rem(f, 2)
+    share = 5 - 2 * lax.rem(f, 2)
 
     def done(s):
-        return 1 + (s * share + 9 - 2 * share) // 3
+        return (s * share + 12 - 2 * share) // 3
 
     with scope("ld0"):
         loads[0].wait()
@@ -264,11 +264,24 @@
         ours(1)
 
     def slot(s):
-        loop(done(s) + AHEAD, done(s + 1) + AHEAD, exchange)
+        def exchange_next():
+            loop(done(s) + AHEAD, done(s + 1) + AHEAD, exchange)
+
+        pl.when(s < half - 1)(exchange_next)
 
         with scope("ag"):
             gather_step(s)
 
+        pl.when(s == half - 1)(exchange_next)
+
+        @pl.when(s == half - 1)
+        def _():
+            take(full.at[0, z, 1 - par], pair_recv)
+            for load in loads[4:]:
+                load.wait()
+            with scope("grad"):
+                loop(0, 2, gradient)
+
         @pl.when(s < 2)
         def _():
             with scope("early"):
@@ -281,28 +294,23 @@
 
     loop(0, half, slot)
     last = done(half)
-    loop(last + AHEAD, planes + 2, exchange)
-    take(full.at[0, z, 1 - par], pair_recv)
-    for load in loads[4:]:
-        load.wait()
-
-    def after(g):
-        @pl.when(g > 0)
-        def _():
-            with scope("rs"):
-                ring_step(last - 1 + g)
-
-        @pl.when(g == 1)
+
+    def after(r):
+        @pl.when(r + AHEAD < planes + 2)
+        def _():
+            exchange(r + AHEAD)
+
+        @pl.when(r == last + lax.rem(f, 2))
         def _():
             with scope("across"):
                 take(full.at[1, :, 1 - par], ya_recv)
-
-        @pl.when(g < 3)
-        def _():
             with scope("grad"):
-                loop((3 * g + 1) // 2, g + 2, gradient)
-
-    loop(0, planes - last + 1, after)
+                loop(2, 4, gradient)
+
+        with scope("rs"):
+            ring_step(r)
+
+    loop(last, planes, after)
 
     with scope("rs_last"):
         for h in range(2):
@@ -380,11 +388,11 @@
             pltpu.SMEM(kept_blocks.shape[-1:], jnp.int32),
             dma((6,)),
             dma, dma,
-            dma((3,)), dma((3, 2, half)),
+            dma((3,)), dma((3, 2, 3)),
             dma, dma,
             dma, dma((2, half + 1)),
             dma, dma((2, 2, 2)),
-            dma, dma((2, 2, half - 2, 2)),
+            dma, dma((2, 2, 3, 2)),
             dma, dma,
         ],
         compiler_params=pltpu.CompilerParams(

time: 57.8 us -> 56.6 us (0.979)
  Pallas kernels: 56.4 us -> 55.2 us
    pallas_call x1, Pallas kernels: 55.2 us -> 54 us  [body(): pl.pallas_call(kernel, out_shape=(pltpu.VMEM((rows, width), BF16), pltpu....]
where the time goes in v5:
time: 56.6 us; the launch traced here: 56.5 us
  Pallas kernels  55.2 us (98%)
  between operations  1.29 us (2%)
    pallas_call x1, Pallas kernels, body(): pl.pallas_call(kernel, out_shape=(pltpu.VMEM((rows, width), BF16), pltpu....  54 us
    pallas_call x1, Pallas kernels, body(): pl.pallas_call(place, out_shape=tuple((jax.ShapeDtypeStruct(x.shape, x.dt...  1.18 us

profile of v5, /device:TPU:16, one launch (start us, length us, event | category | flops | bytes accessed | tf_op | source)
XLA Modules:
  0.0 56.5 jit_solution(5731277140812337420)
XLA Ops:
  1.3 54.0 %shard_map.85 = (bf16[32,1024]{1,0:T(8,128)(2,1)S(1)}, bf16[1024,512]{1,0:T(8,128)(2,1)S(1)}, f32[1024,128]{1,0:T(8,128)S(1)}) custom-call(f32[1]{0:T(128)S(6)} %copy.9.step_ref, s32[8]{0:T(128)} %bitcast.7, bf16[32,1024]{1,0:T(8,128)(2,1)} %acts_ref.1, bf16[16,2,32,512]{3,2,1,0:T(8,128)(2,1)} %bitcast.5, bf16[1024,512]{1,0:T(8,128)(2,1)} %w_hbm.1, ...), custom_call_target="tpu_custom_call" | custom-call | tf_op jit(solution)/shard_map/pallas_call | solution.py:366
  55.3 1.2 %shard_map.86 = (bf16[32,1024]{1,0:T(8,128)(2,1)}, bf16[1024,512]{1,0:T(8,128)(2,1)}, f32[1024,128]{1,0:T(8,128)}) custom-call(bf16[32,1024]{1,0:T(8,128)(2,1)S(1)} %get-tuple-element.9.ig_in, bf16[1024,512]{1,0:T(8,128)(2,1)S(1)} %get-tuple-element.10.ro_in, f32[1024,128]{1,0:T(8,128)S(1)} %get-tuple-element.11.ow_in), custom_call_target="tpu_custom_call" | custom-call | tf_op jit(solution)/shard_map/pallas_call | solution.py:411

commit v6 on v5

--- a/solution.py
+++ b/solution.py
@@ -173,21 +173,25 @@
         exchanged(h, k, 2)
         for d in range(2):
             p = plane(z + sign[d] * k)
-
-            @pl.when(k == half - 2)
-            def _():
+            own[p, h] = own[p, h] + yin[p, h].astype(F32)
+
+        @pl.when(k == half - 2)
+        def _():
+            for d in range(2):
+                p = plane(z + sign[d] * k)
                 take(ring16.at[d, h, 1], re_recv.at[d, h, 1])
                 own[p, h] = own[p, h] + ring16[d, h, 1].astype(F32)
 
-            for i in range(2):
-                lines = pl.ds(i * part, part)
+        for i in range(2):
+            lines = pl.ds(i * part, part)
+            for d in range(2):
+                p = plane(z + sign[d] * k)
 
                 @pl.when(k < half - 2)
                 def _():
                     take(ring.at[d, h, k, lines], rs_recv.at[d, h, lax.rem(k, 3), i])
                     own[p, h, lines] = own[p, h, lines] + ring[d, h, k, lines]
 
-                own[p, h, lines] = own[p, h, lines] + yin[p, h, lines].astype(F32)
                 remote(
                     own.at[p, h, lines], ring.at[d, h, k - 1, lines],
                     rs_send, rs_recv.at[d, h, lax.rem(k - 1, 3), i], zdev[d],

time: 56.6 us -> 56.6 us (level)
  no operation moved by 1% of the time
where the time goes in v6:
time: 56.6 us; the launch traced here: 56.5 us
  Pallas kernels  55.2 us (98%)
  between operations  1.29 us (2%)
    pallas_call x1, Pallas kernels, body(): pl.pallas_call(kernel, out_shape=(pltpu.VMEM((rows, width), BF16), pltpu....  54 us
    pallas_call x1, Pallas kernels, body(): pl.pallas_call(place, out_shape=tuple((jax.ShapeDtypeStruct(x.shape, x.dt...  1.18 us

profile of v6, /device:TPU:16, one launch (start us, length us, event | category | flops | bytes accessed | tf_op | source)
XLA Modules:
  0.0 56.5 jit_solution(4857807093179481548)
XLA Ops:
  1.3 54.0 %shard_map.85 = (bf16[32,1024]{1,0:T(8,128)(2,1)S(1)}, bf16[1024,512]{1,0:T(8,128)(2,1)S(1)}, f32[1024,128]{1,0:T(8,128)S(1)}) custom-call(f32[1]{0:T(128)S(6)} %copy.9.step_ref, s32[8]{0:T(128)} %bitcast.7, bf16[32,1024]{1,0:T(8,128)(2,1)} %acts_ref.1, bf16[16,2,32,512]{3,2,1,0:T(8,128)(2,1)} %bitcast.5, bf16[1024,512]{1,0:T(8,128)(2,1)} %w_hbm.1, ...), custom_call_target="tpu_custom_call" | custom-call | tf_op jit(solution)/shard_map/pallas_call | solution.py:370
  55.3 1.2 %shard_map.86 = (bf16[32,1024]{1,0:T(8,128)(2,1)}, bf16[1024,512]{1,0:T(8,128)(2,1)}, f32[1024,128]{1,0:T(8,128)}) custom-call(bf16[32,1024]{1,0:T(8,128)(2,1)S(1)} %get-tuple-element.9.ig_in, bf16[1024,512]{1,0:T(8,128)(2,1)S(1)} %get-tuple-element.10.ro_in, f32[1024,128]{1,0:T(8,128)S(1)} %get-tuple-element.11.ow_in), custom_call_target="tpu_custom_call" | custom-call | tf_op jit(solution)/shard_map/pallas_call | solution.py:415
